TPU v7x, 256 devices: a whole 4x4x8 slice. The times are simulated.
256 devices in a mesh: row: 64 (over z, y, core), col: 4 (over x).
Axes of the slice: x: 4, y: 4, z: 8, core: 2. Of those that a mesh axis runs over, the one named last changes fastest.
Arguments:
- train_points: float32 [16, 3, 64, 128], P(None, None, 'row'), may hold values from -6 to 6
- new_points: float32 [16, 256], replicated, may hold values from -6 to 6
- lengthscales: float32 [16], replicated, may hold values from 2.5 to 6
- factor: float32 [3, 64, 128, 3, 4, 2048], P(None, 'row', None, None, 'col'), may hold values from -0.02734375 to 0.02734375
- diag_inverse: float32 [3, 64, 128, 4, 2048], P(None, 'row', None, 'col'), may hold values from -3 to 3
Outputs:
- solution: float32 [3, 4, 64, 32, 256], P(None, 'col', 'row')
All inputs are finite; a program needn't handle non-finite values.
Results may differ from a plain program's by a relative error of at most 0.0001.
Values sent between devices are 32-bit elements; how exact they have to be, the bound alone decides.
No kernel may reach another device: no remote copies, remote signals or barrier semaphores. Data moves between devices by JAX's collectives and lax.ppermute only.
A program may use at most 128 MiB of HBM per device.

v0:
```python
import jax
import jax.numpy as jnp
from jax import lax
from jax.sharding import PartitionSpec as P


def on_device(train_points, new_points, lengthscales, factor, diag_inverse):
    highest = lax.Precision.HIGHEST
    panels = factor.shape[0]
    block_rows = factor.shape[2]
    quarter_cols = factor.shape[5]
    new_count = new_points.shape[1]
    share_rows = block_rows // lax.axis_size("col")
    scaled_train = (train_points / lengthscales[:, None, None, None]).reshape(
        train_points.shape[0], panels * block_rows
    )
    scaled_new = new_points / lengthscales[:, None]
    inner_products = jnp.dot(scaled_train.T, scaled_new, precision=highest)
    sqdist = (
        jnp.sum(scaled_train * scaled_train, axis=0)[:, None]
        + jnp.sum(scaled_new * scaled_new, axis=0)[None, :]
        - 2.0 * inner_products
    )
    kernel = jnp.exp(-0.5 * sqdist).reshape(panels, block_rows, new_count)
    factor_blocks = factor.reshape(panels, block_rows, panels, quarter_cols)
    inverse_blocks = diag_inverse.reshape(panels, block_rows, quarter_cols)
    panel_numbers = jnp.arange(panels)

    def update(partial_rows, panel, quarter, after):
        column_slab = lax.dynamic_index_in_dim(factor_blocks, panel, axis=2, keepdims=False)
        change = jnp.einsum("piq,qm->pim", column_slab, quarter, precision=highest)
        below = (panel_numbers > after)[:, None, None]
        return partial_rows + jnp.where(below, change, 0.0)

    def advance(panel, loop_state):
        partial_rows, solved, pending = loop_state
        own_partial = lax.dynamic_index_in_dim(partial_rows, panel, 0, keepdims=False)
        summed = lax.psum(own_partial, "col")
        residual = lax.dynamic_index_in_dim(kernel, panel, 0, keepdims=False) - summed
        inverse_block = lax.dynamic_index_in_dim(inverse_blocks, panel, 0, keepdims=False)
        product = jnp.einsum("iq,im->qm", inverse_block, residual, precision=highest)
        own_rows = lax.psum_scatter(product, "row", scatter_dimension=0, tiled=True)
        quarter = lax.all_gather(own_rows, "row", axis=0, tiled=True)
        solved = lax.dynamic_update_index_in_dim(solved, own_rows, panel, 0)
        partial_rows = update(partial_rows, panel, quarter, panel)
        return (partial_rows, solved, pending)

    initial = (
        jnp.zeros((panels, block_rows, new_count), jnp.float32),
        jnp.zeros((panels, share_rows, new_count), jnp.float32),
        jnp.zeros((quarter_cols, new_count), jnp.float32),
    )
    partial_rows, solved, pending = lax.fori_loop(0, panels, advance, initial)
    return solved.reshape(panels, 1, 1, share_rows, new_count)


def solution(mesh):
    return jax.shard_map(
        on_device,
        mesh=mesh,
        in_specs=(
            P(None, None, "row", None),
            P(),
            P(),
            P(None, "row", None, None, "col", None),
            P(None, "row", None, "col", None),
        ),
        out_specs=P(None, "col", "row", None, None),
        check_vma=False,
    )
```

profile of v0, /device:TPU:1, one launch (start us, length us, event | category | flops | bytes accessed | tf_op | source)
XLA Modules:
  0.0 868.2 jit_solution(1024487664733539460)
XLA Ops:
  6.5 0.9 fusion.27
  7.4 0.8 multiply_reduce_fusion.1
  8.3 2.0 fusion.24
  10.3 12.1 %copy.15 = f32[3,1,128,3,1,2048]{5,2,0,3,4,1:T(8,128)} copy(f32[3,1,128,3,1,2048]{5,4,3,2,1,0:T(1,128)} %param.10) | data formatting | bytes 18874368 | tf_op args[3]
  22.4 1.4 copy.16
  23.8 837.8 %while.16 = (s32[]{:T(128)}, f32[3,128,256]{2,1,0:T(8,128)}, f32[3,32,256]{2,1,0:T(8,128)}, f32[3,128,3,2048]{3,1,0,2:T(8,128)}, f32[3,128,2048]{2,1,0:T(8,128)S...) while((s32[]{:T(128)}, f32[3,128,256]{2,1,0:T(8,128)}, f32[3,32,256]{2,1,0:T(8,128)}, ...), condition=%wide.region_5.6_spmd.clone, body=%wide.region_2.5_spmd.clone.sunk | while | flops 3221585920 | bytes 24118516 | solution.py:53
  24.1 0.7 dynamic-slice_bitcast_fusion.2
  24.9 50.3 %all-reduce.2.cloned.1.call-done = f32[128,256]{1,0:T(8,128)} async-done(((f32[128,256]{1,0:T(8,128)}), f32[128,256]{1,0:T(8,128)}) %all-reduce.2.cloned.1.call-update) | async-done | bytes 131088 | tf_op jit(solution)/shard_map/while/body/eval_jaxpr/psum | solution.py:38
  75.2 4.1 fusion.36
  79.3 0.0 all-gather.2.cloned.1.call-start
  79.4 138.6 %reduce-scatter.2.cloned.1.call-done = f32[32,256]{1,0:T(8,128)} async-done(((f32[2048,256]{1,0:T(8,128)}), f32[32,256]{1,0:T(8,128)}) %reduce-scatter.2.cloned.1.call-update) | async-done | bytes 32784 | tf_op jit(solution)/shard_map/while/body/eval_jaxpr/reduce_scatter | solution.py:42
  218.1 1.4 bitcast_dynamic-update-slice_fusion.2
  219.4 82.4 %all-gather.2.cloned.1.call-done = f32[2048,256]{1,0:T(8,128)} async-done(((f32[32,256]{1,0:T(8,128)}), f32[2048,256]{1,0:T(8,128)}) %all-gather.2.cloned.1.call-update) | async-done | bytes 2097168 | tf_op jit(solution)/shard_map/while/body/eval_jaxpr/all_gather | solution.py:43
  301.9 6.0 fusion.37
  307.8 1.0 broadcast_select_fusion.2
  308.9 0.7 dynamic-slice_bitcast_fusion.2
  309.6 42.5 %all-reduce.2.cloned.1.call-done = f32[128,256]{1,0:T(8,128)} async-done(((f32[128,256]{1,0:T(8,128)}), f32[128,256]{1,0:T(8,128)}) %all-reduce.2.cloned.1.call-update) | async-done | bytes 131088 | tf_op jit(solution)/shard_map/while/body/eval_jaxpr/psum | solution.py:38
  352.1 4.1 fusion.36
  356.2 0.0 all-gather.2.cloned.1.call-start
  356.3 138.2 %reduce-scatter.2.cloned.1.call-done = f32[32,256]{1,0:T(8,128)} async-done(((f32[2048,256]{1,0:T(8,128)}), f32[32,256]{1,0:T(8,128)}) %reduce-scatter.2.cloned.1.call-update) | async-done | bytes 32784 | tf_op jit(solution)/shard_map/while/body/eval_jaxpr/reduce_scatter | solution.py:42
  494.5 1.4 bitcast_dynamic-update-slice_fusion.2
  495.9 82.6 %all-gather.2.cloned.1.call-done = f32[2048,256]{1,0:T(8,128)} async-done(((f32[32,256]{1,0:T(8,128)}), f32[2048,256]{1,0:T(8,128)}) %all-gather.2.cloned.1.call-update) | async-done | bytes 2097168 | tf_op jit(solution)/shard_map/while/body/eval_jaxpr/all_gather | solution.py:43
  578.5 6.0 fusion.37
  584.5 1.0 broadcast_select_fusion.2
  585.5 0.7 dynamic-slice_bitcast_fusion.2
  586.2 42.8 %all-reduce.2.cloned.1.call-done = f32[128,256]{1,0:T(8,128)} async-done(((f32[128,256]{1,0:T(8,128)}), f32[128,256]{1,0:T(8,128)}) %all-reduce.2.cloned.1.call-update) | async-done | bytes 131088 | tf_op jit(solution)/shard_map/while/body/eval_jaxpr/psum | solution.py:38
  629.0 4.1 fusion.36
  633.2 0.0 all-gather.2.cloned.1.call-start
  633.2 138.6 %reduce-scatter.2.cloned.1.call-done = f32[32,256]{1,0:T(8,128)} async-done(((f32[2048,256]{1,0:T(8,128)}), f32[32,256]{1,0:T(8,128)}) %reduce-scatter.2.cloned.1.call-update) | async-done | bytes 32784 | tf_op jit(solution)/shard_map/while/body/eval_jaxpr/reduce_scatter | solution.py:42
  771.9 1.4 bitcast_dynamic-update-slice_fusion.2
  773.3 82.4 %all-gather.2.cloned.1.call-done = f32[2048,256]{1,0:T(8,128)} async-done(((f32[32,256]{1,0:T(8,128)}), f32[2048,256]{1,0:T(8,128)}) %all-gather.2.cloned.1.call-update) | async-done | bytes 2097168 | tf_op jit(solution)/shard_map/while/body/eval_jaxpr/all_gather | solution.py:43
  855.7 6.0 fusion.37
  (23 shorter events, 0.4 us)
Async XLA Ops:
  10.3 12.1 %copy-start = (f32[3,1,128,1,2048]{4,3,2,1,0:T(1,128)S(1)}, f32[3,1,128,1,2048]{4,3,2,1,0:T(1,128)}, u32[]{:S(2)}) copy-start(f32[3,1,128,1,2048]{4,3,2,1,0:T(1,128)} %param.11) | copy-start | bytes 9437188
  24.0 51.2 %all-reduce.2.cloned.1.call-start = ((), (), s32[]{:S(2)}) async-start(), calls=%async_computation.1 | async-start | bytes 262144 | tf_op jit(solution)/shard_map/while/body/eval_jaxpr/psum | solution.py:38
  24.8 193.2 %reduce-scatter.2.cloned.1.call-start = ((), (), s32[]{:S(2)}) async-start(), calls=%async_computation.2 | async-start | bytes 2129920 | tf_op jit(solution)/shard_map/while/body/eval_jaxpr/reduce_scatter | solution.py:42
  79.3 222.5 %all-gather.2.cloned.1.call-start = ((), (), s32[]{:S(2)}) async-start(), calls=%async_computation.3 | async-start | bytes 2129920 | tf_op jit(solution)/shard_map/while/body/eval_jaxpr/all_gather | solution.py:43
  307.8 44.3 %all-reduce.2.cloned.1.call-start = ((), (), s32[]{:S(2)}) async-start(), calls=%async_computation.1 | async-start | bytes 262144 | tf_op jit(solution)/shard_map/while/body/eval_jaxpr/psum | solution.py:38
  309.6 184.9 %reduce-scatter.2.cloned.1.call-start = ((), (), s32[]{:S(2)}) async-start(), calls=%async_computation.2 | async-start | bytes 2129920 | tf_op jit(solution)/shard_map/while/body/eval_jaxpr/reduce_scatter | solution.py:42
  356.2 222.2 %all-gather.2.cloned.1.call-start = ((), (), s32[]{:S(2)}) async-start(), calls=%async_computation.3 | async-start | bytes 2129920 | tf_op jit(solution)/shard_map/while/body/eval_jaxpr/all_gather | solution.py:43
  584.4 44.6 %all-reduce.2.cloned.1.call-start = ((), (), s32[]{:S(2)}) async-start(), calls=%async_computation.1 | async-start | bytes 262144 | tf_op jit(solution)/shard_map/while/body/eval_jaxpr/psum | solution.py:38
  586.2 185.7 %reduce-scatter.2.cloned.1.call-start = ((), (), s32[]{:S(2)}) async-start(), calls=%async_computation.2 | async-start | bytes 2129920 | tf_op jit(solution)/shard_map/while/body/eval_jaxpr/reduce_scatter | solution.py:42
  633.2 222.5 %all-gather.2.cloned.1.call-start = ((), (), s32[]{:S(2)}) async-start(), calls=%async_computation.3 | async-start | bytes 2129920 | tf_op jit(solution)/shard_map/while/body/eval_jaxpr/all_gather | solution.py:43
Sparse Core Ops, SparseCore 0:
  27.2 47.9 all-reduce.1
  79.8 138.1 reduce-scatter.1
  220.8 81.0 all-gather.1
  310.7 41.4 all-reduce.1
  356.6 137.9 reduce-scatter.1
  497.1 81.3 all-gather.1
  587.6 41.4 all-reduce.1
  633.6 138.1 reduce-scatter.1
  774.6 81.0 all-gather.1
where the time goes:
time: 869 us; the launch traced here: 868 us
  waiting for transfers between devices  799 us (92%)
  matrix products  32.3 us (4%)
  local copies, waits for them, and re-layouts  19.7 us (2%)
  between operations  13.1 us (2%)
    reduce_scatter x3, waiting for transfers between devices, advance(): own_rows = lax.psum_scatter(product, 'row', scatter_dimension=0, tiled=True)  415 us
    all_gather x3, waiting for transfers between devices, advance(): quarter = lax.all_gather(own_rows, 'row', axis=0, tiled=True)  247 us
    psum x3, waiting for transfers between devices, advance(): summed = lax.psum(own_partial, 'col')  136 us
    dot_general x3, matrix products, update(): change = jnp.einsum('piq,qm->pim', column_slab, quarter, precision=highest)  17.9 us
  transfers between devices with their start and end apart: 9, of which 9 were waited for; matrix products, arithmetic and copies ran while one was open for 0% of the time, Pallas kernels for 0%

commit v1 on v0

--- a/solution.py
+++ b/solution.py
@@ -2,6 +2,15 @@
 import jax.numpy as jnp
 from jax import lax
 from jax.sharding import PartitionSpec as P
+
+
+def sum_by_hops(x, mesh_axis):
+    size = lax.axis_size(mesh_axis)
+    acc, far = (x, 1)
+    while far < size:
+        acc = acc + lax.ppermute(acc, mesh_axis, [(i, i ^ far) for i in range(size)])
+        far = 2 * far
+    return acc
 
 
 def on_device(train_points, new_points, lengthscales, factor, diag_inverse):
@@ -35,7 +44,7 @@
     def advance(panel, loop_state):
         partial_rows, solved, pending = loop_state
         own_partial = lax.dynamic_index_in_dim(partial_rows, panel, 0, keepdims=False)
-        summed = lax.psum(own_partial, "col")
+        summed = sum_by_hops(own_partial, "col")
         residual = lax.dynamic_index_in_dim(kernel, panel, 0, keepdims=False) - summed
         inverse_block = lax.dynamic_index_in_dim(inverse_blocks, panel, 0, keepdims=False)
         product = jnp.einsum("iq,im->qm", inverse_block, residual, precision=highest)

time: 869 us -> 759 us (0.87)
  waiting for transfers between devices: 799 us -> 677 us
  starting transfers between devices: 0.3 us -> 14 us
    psum x3 -> x0, waiting for transfers between devices: 136 us -> none  [advance(): summed = lax.psum(own_partial, 'col')]
    ppermute x0 -> x6, waiting for transfers between devices: none -> 17.3 us  [sum_by_hops(): lax.ppermute(acc, mesh_axis, [(i, i ^ far) for i in range(size)])]
    ppermute x0 -> x6, starting transfers between devices: none -> 13.9 us  [sum_by_hops(): lax.ppermute(acc, mesh_axis, [(i, i ^ far) for i in range(size)])]
  transfers between devices with their start and end apart: 9 -> 12, of which waited for: 9 -> 12; matrix products, arithmetic and copies ran while one was open for 0% -> 1% of each run, Pallas kernels for 0% -> 0%
where the time goes in v1:
time: 759 us; the launch traced here: 758 us
  waiting for transfers between devices  677 us (89%)
  matrix products  32.1 us (4%)
  local copies, waits for them, and re-layouts  17.7 us (2%)
  starting transfers between devices  14 us (2%)
  between operations  13.4 us (2%)
    reduce_scatter x3, waiting for transfers between devices, advance(): own_rows = lax.psum_scatter(product, 'row', scatter_dimension=0, tiled=True)  410 us
    all_gather x3, waiting for transfers between devices, advance(): quarter = lax.all_gather(own_rows, 'row', axis=0, tiled=True)  249 us
    dot_general x3, matrix products, update(): change = jnp.einsum('piq,qm->pim', column_slab, quarter, precision=highest)  17.9 us
    ppermute x6, waiting for transfers between devices, sum_by_hops(): lax.ppermute(acc, mesh_axis, [(i, i ^ far) for i in range(size)])  17.3 us
  transfers between devices with their start and end apart: 12, of which 12 were waited for; matrix products, arithmetic and copies ran while one was open for 1% of the time, Pallas kernels for 0%

profile of v1, /device:TPU:1, one launch (start us, length us, event | category | flops | bytes accessed | tf_op | source)
XLA Modules:
  0.0 758.1 jit_solution(14000335803166460265)
XLA Ops:
  8.3 2.0 fusion.25
  10.3 12.1 %copy.15 = f32[3,1,128,3,1,2048]{5,2,0,3,4,1:T(8,128)} copy(f32[3,1,128,3,1,2048]{5,4,3,2,1,0:T(1,128)} %param.10) | data formatting | bytes 18874368 | tf_op args[3]
  22.4 1.4 copy.16
  23.8 727.4 %while.16 = (s32[]{:T(128)}, f32[3,128,256]{2,1,0:T(8,128)}, f32[3,32,256]{2,1,0:T(8,128)}, f32[3,128,3,2048]{3,1,0,2:T(8,128)}, f32[3,128,2048]{2,1,0:T(8,128)S...) while((s32[]{:T(128)}, f32[3,128,256]{2,1,0:T(8,128)}, f32[3,32,256]{2,1,0:T(8,128)}, ...), condition=%wide.region_4.5_spmd.clone, body=%wide.region_2.4_spmd.clone.sunk | while | flops 3221618688 | bytes 24904992 | solution.py:62
  24.2 2.1 collective-permute-start
  26.3 2.4 collective-permute-done
  28.7 3.6 collective-permute-start.1
  32.3 2.4 collective-permute-done.1
  34.7 4.1 fusion.40
  38.8 140.9 %reduce-scatter.2.cloned.1.call-done = f32[32,256]{1,0:T(8,128)} async-done(((f32[2048,256]{1,0:T(8,128)}), f32[32,256]{1,0:T(8,128)}) %reduce-scatter.2.cloned.1.call-update) | async-done | bytes 32784 | tf_op jit(solution)/shard_map/while/body/eval_jaxpr/reduce_scatter | solution.py:51
  179.7 1.4 bitcast_dynamic-update-slice_fusion.2
  181.1 82.9 %all-gather.2.cloned.1.call-done = f32[2048,256]{1,0:T(8,128)} async-done(((f32[32,256]{1,0:T(8,128)}), f32[2048,256]{1,0:T(8,128)}) %all-gather.2.cloned.1.call-update) | async-done | bytes 2097168 | tf_op jit(solution)/shard_map/while/body/eval_jaxpr/all_gather | solution.py:52
  264.0 6.0 fusion.41
  270.0 1.0 broadcast_select_fusion.2
  271.1 1.3 collective-permute-start
  272.3 3.7 collective-permute-done
  276.0 2.8 collective-permute-start.1
  278.8 2.6 collective-permute-done.1
  281.4 4.1 fusion.40
  285.6 134.6 %reduce-scatter.2.cloned.1.call-done = f32[32,256]{1,0:T(8,128)} async-done(((f32[2048,256]{1,0:T(8,128)}), f32[32,256]{1,0:T(8,128)}) %reduce-scatter.2.cloned.1.call-update) | async-done | bytes 32784 | tf_op jit(solution)/shard_map/while/body/eval_jaxpr/reduce_scatter | solution.py:51
  420.2 1.4 bitcast_dynamic-update-slice_fusion.2
  421.6 83.1 %all-gather.2.cloned.1.call-done = f32[2048,256]{1,0:T(8,128)} async-done(((f32[32,256]{1,0:T(8,128)}), f32[2048,256]{1,0:T(8,128)}) %all-gather.2.cloned.1.call-update) | async-done | bytes 2097168 | tf_op jit(solution)/shard_map/while/body/eval_jaxpr/all_gather | solution.py:52
  504.7 6.0 fusion.41
  511.7 1.3 collective-permute-start
  513.0 3.7 collective-permute-done
  516.6 2.8 collective-permute-start.1
  519.4 2.6 collective-permute-done.1
  522.1 4.1 fusion.40
  526.2 134.9 %reduce-scatter.2.cloned.1.call-done = f32[32,256]{1,0:T(8,128)} async-done(((f32[2048,256]{1,0:T(8,128)}), f32[32,256]{1,0:T(8,128)}) %reduce-scatter.2.cloned.1.call-update) | async-done | bytes 32784 | tf_op jit(solution)/shard_map/while/body/eval_jaxpr/reduce_scatter | solution.py:51
  661.1 1.4 bitcast_dynamic-update-slice_fusion.2
  662.5 82.8 %all-gather.2.cloned.1.call-done = f32[2048,256]{1,0:T(8,128)} async-done(((f32[32,256]{1,0:T(8,128)}), f32[2048,256]{1,0:T(8,128)}) %all-gather.2.cloned.1.call-update) | async-done | bytes 2097168 | tf_op jit(solution)/shard_map/while/body/eval_jaxpr/all_gather | solution.py:52
  745.3 6.0 fusion.41
  (29 shorter events, 3.2 us)
Async XLA Ops:
  10.3 12.1 %copy-start = (f32[3,1,128,1,2048]{4,3,2,1,0:T(1,128)S(1)}, f32[3,1,128,1,2048]{4,3,2,1,0:T(1,128)}, u32[]{:S(2)}) copy-start(f32[3,1,128,1,2048]{4,3,2,1,0:T(1,128)} %param.11) | copy-start | bytes 9437188
  24.0 155.7 %reduce-scatter.2.cloned.1.call-start = ((), (), s32[]{:S(2)}) async-start(), calls=%async_computation.1 | async-start | bytes 2129920 | tf_op jit(solution)/shard_map/while/body/eval_jaxpr/reduce_scatter | solution.py:51
  24.2 4.5 collective-permute-start
  28.7 6.0 collective-permute-start.1
  38.7 225.3 %all-gather.2.cloned.1.call-start = ((), (), s32[]{:S(2)}) async-start(), calls=%async_computation.2 | async-start | bytes 2129920 | tf_op jit(solution)/shard_map/while/body/eval_jaxpr/all_gather | solution.py:52
  270.0 150.1 %reduce-scatter.2.cloned.1.call-start = ((), (), s32[]{:S(2)}) async-start(), calls=%async_computation.1 | async-start | bytes 2129920 | tf_op jit(solution)/shard_map/while/body/eval_jaxpr/reduce_scatter | solution.py:51
  271.1 4.9 collective-permute-start
  276.0 5.4 collective-permute-start.1
  285.5 219.2 %all-gather.2.cloned.1.call-start = ((), (), s32[]{:S(2)}) async-start(), calls=%async_computation.2 | async-start | bytes 2129920 | tf_op jit(solution)/shard_map/while/body/eval_jaxpr/all_gather | solution.py:52
  510.6 150.5 %reduce-scatter.2.cloned.1.call-start = ((), (), s32[]{:S(2)}) async-start(), calls=%async_computation.1 | async-start | bytes 2129920 | tf_op jit(solution)/shard_map/while/body/eval_jaxpr/reduce_scatter | solution.py:51
  511.7 4.9 collective-permute-start
  516.6 5.4 collective-permute-start.1
  526.1 219.1 %all-gather.2.cloned.1.call-start = ((), (), s32[]{:S(2)}) async-start(), calls=%async_computation.2 | async-start | bytes 2129920 | tf_op jit(solution)/shard_map/while/body/eval_jaxpr/all_gather | solution.py:52
Sparse Core Ops, SparseCore 0:
  38.9 140.7 reduce-scatter.1
  182.8 81.1 all-gather.1
  285.6 134.4 reduce-scatter.1
  423.1 81.4 all-gather.1
  526.3 134.7 reduce-scatter.1
  664.1 81.1 all-gather.1
